TPU v7x, 32 devices: a whole 2x2x4 slice. The times are simulated.
32 devices in a mesh: leaf: 4 (over y, core), panel: 8 (over z, x).
Axes of the slice: x: 2, y: 2, z: 4, core: 2. Of those that a mesh axis runs over, the one named last changes fastest.
Arguments:
- pivot_rhs: float32 [4, 48, 4096], P('leaf', None, 'panel'), may hold values from -6 to 6
- subtree_update: float32 [4, 64, 4096], P('leaf', None, 'panel'), may hold values from -6 to 6
- lower_pivot: bfloat16 [2, 4, 4096, 4096], P(None, 'leaf', 'panel'), as said below
- lower_update: bfloat16 [2, 4, 4096, 4096], P(None, 'leaf', None, 'panel'), as said below
- row_map: int32 [2, 4, 2, 4096], P(None, 'leaf', None, 'panel'), may hold values from 0 to 1023, as said below
- root_inverse: bfloat16 [4096, 4096], P('panel'), as said below
Outputs:
- pivot_solution: float32 [4, 48, 4096], P('leaf', None, 'panel')
- subtree_solution: float32 [4, 64, 4096], P('leaf', None, 'panel')
Inputs may be any that keep to these rules, and one draw needn't show every extreme that they name: row_map[l, i] is the same for all i that share i >> (l + 1); within one panel block of 512 rows of one child the values are distinct. lower_pivot[l, i] is the same for all i that share i >> (l + 1), and is zero above its diagonal blocks of 512 rows. lower_update[l, i] is the same for all i that share i >> (l + 1). root_inverse is symmetric.
All inputs are finite; a program needn't handle non-finite values.
Results may differ from a plain program's by a relative error of at most 0.0003.
Values sent between devices are 32-bit elements; how exact they have to be, the bound alone decides.
A program may use at most 64 MiB of HBM per device.

v0:
```python
import jax
import jax.numpy as jnp
from jax import lax
from jax.sharding import PartitionSpec as P

HIGHEST_PRECISION = lax.Precision.HIGHEST
CONTRACT_LAST = (((1,), (1,)), ((), ()))
CONTRACT_FIRST_LAST = (((0,), (1,)), ((), ()))


def partner(value, axis, stride):
    return lax.ppermute(value, axis, [(i, i ^ 1 << stride) for i in range(lax.axis_size(axis))])


def local(pivot_rhs, subtree_update, lower_pivot, lower_update, row_map, root_inverse):
    levels = lax.axis_size("leaf").bit_length() - 1
    leaf_index = lax.axis_index("leaf")
    pivot_block = pivot_rhs.shape[2]
    update_block = subtree_update.shape[2]
    slot_count = pivot_block + update_block
    current = subtree_update[0]
    solved_levels = []
    onehot_tables = []
    leaf_bits = []
    offset = 0
    for tree_level in range(levels):
        leaf_bit = leaf_index >> tree_level & 1
        col_count = current.shape[0] // 2
        halves = current.reshape(col_count, 2, update_block)
        kept_half = jnp.where(leaf_bit == 0, halves[:, 0], halves[:, 1])
        sent_half = jnp.where(leaf_bit == 0, halves[:, 1], halves[:, 0])
        received = partner(sent_half, "leaf", tree_level)
        children = jnp.where(
            leaf_bit == 0,
            jnp.concatenate([kept_half, received], 1),
            jnp.concatenate([received, kept_half], 1),
        )
        maps = row_map[tree_level, 0].reshape(2 * update_block)
        onehot_table = (maps[:, None] == jnp.arange(slot_count, dtype=jnp.int32)[None, :]).astype(
            jnp.float32
        )
        assembled = jnp.dot(children, onehot_table, precision=HIGHEST_PRECISION)
        right_side = pivot_rhs[0, offset : offset + col_count] + assembled[:, :pivot_block]
        offset = offset + col_count
        inverse_rows = lower_pivot[tree_level, 0]
        update_cols = lower_update[tree_level, 0]
        inverse_cols = inverse_rows.astype(jnp.float32)
        solved = lax.dot_general(
            lax.all_gather(right_side, "panel", axis=1, tiled=True),
            inverse_cols,
            CONTRACT_LAST,
            precision=HIGHEST_PRECISION,
        )
        factor_rows = update_cols.astype(jnp.float32)
        coupled_update = lax.psum_scatter(
            lax.dot_general(factor_rows, solved, CONTRACT_LAST, precision=HIGHEST_PRECISION),
            "panel",
            scatter_dimension=0,
            tiled=True,
        ).T
        current = assembled[:, pivot_block:] - coupled_update
        solved_levels.append(solved)
        onehot_tables.append(onehot_table)
        leaf_bits.append(leaf_bit)
    root_inverse_cols = root_inverse.astype(jnp.float32)
    known = lax.dot_general(
        lax.all_gather(current, "panel", axis=1, tiled=True),
        root_inverse_cols,
        CONTRACT_LAST,
        precision=HIGHEST_PRECISION,
    )
    pieces = [None] * levels
    for tree_level in range(levels - 1, -1, -1):
        inverse_rows = lower_pivot[tree_level, 0]
        update_cols = lower_update[tree_level, 0]
        forward_part = solved_levels[tree_level]
        col_count = forward_part.shape[0]
        known_factor_rows = update_cols.astype(jnp.float32)
        coupling = jnp.dot(
            lax.all_gather(known, "panel", axis=1, tiled=True),
            known_factor_rows,
            precision=HIGHEST_PRECISION,
        )
        residual_part = forward_part - coupling
        pivot_inverse_cols = inverse_rows.astype(jnp.float32)
        own_x = lax.psum_scatter(
            lax.dot_general(
                pivot_inverse_cols, residual_part, CONTRACT_FIRST_LAST, precision=HIGHEST_PRECISION
            ),
            "panel",
            scatter_dimension=0,
            tiled=True,
        ).T
        pieces[tree_level] = own_x
        whole_front = jnp.concatenate([own_x, known], 1)
        children = lax.dot_general(
            whole_front, onehot_tables[tree_level], CONTRACT_LAST, precision=HIGHEST_PRECISION
        )
        leaf_bit = leaf_bits[tree_level]
        first_child = children[:, :update_block]
        second_child = children[:, update_block:]
        own_child = jnp.where(leaf_bit == 0, first_child, second_child)
        sent_child = jnp.where(leaf_bit == 0, second_child, first_child)
        received = partner(sent_child, "leaf", tree_level)
        paired = jnp.where(
            leaf_bit == 0, jnp.stack([own_child, received], 1), jnp.stack([received, own_child], 1)
        )
        known = paired.reshape(2 * col_count, update_block)
    return (jnp.concatenate(pieces, 0)[None], known[None])


def solution(mesh):
    in_specs = (
        P("leaf", None, "panel"),
        P("leaf", None, "panel"),
        P(None, "leaf", "panel", None),
        P(None, "leaf", None, "panel"),
        P(None, "leaf", None, "panel"),
        P("panel", None),
    )
    out_specs = (P("leaf", None, "panel"), P("leaf", None, "panel"))
    return jax.shard_map(local, mesh=mesh, in_specs=in_specs, out_specs=out_specs, check_vma=False)
```

profile of v0, /device:TPU:1, one launch (start us, length us, event | category | flops | bytes accessed | tf_op | source)
XLA Modules:
  0.0 490.3 jit_solution(4684953163303562873)
XLA Ops:
  9.7 1.6 fusion.15
  12.2 26.9 %all_gather.15 = f32[32,4096]{1,0:T(8,128)S(1)} all-gather(f32[32,512]{1,0:T(8,128)S(1)} %slice_add_fusion), channel_id=1, replica_groups=mesh['leaf'=4,'panel'=8] {'panel'}, dimensions={1}, use_global_device_ids=true | all-gather | bytes 589824 | tf_op jit(solution)/shard_map/all_gather | solution.py:49
  39.0 5.9 %fusion.10 = f32[32,512]{1,0:T(8,128)S(1)} fusion(f32[32,4096]{1,0:T(8,128)S(1)} %all_gather.15, bf16[2,1,512,4096]{3,2,1,0:T(8,128)(2,1)} %param.8), kind=kOutput, calls=%fused_computation.14 | convolution fusion | flops 805306368 | bytes 4784128 | tf_op jit(solution)/shard_map/dot_general | solution.py:48
  44.9 6.7 %convolution_bitcast_fusion.1 = f32[4096,32]{0,1:T(8,128)} fusion(f32[32,512]{1,0:T(8,128)S(1)} %fusion.10, bf16[2,1,4096,512]{3,2,1,0:T(8,128)(2,1)} %param.9), kind=kOutput, calls=%fused_computation.1 | convolution fusion | flops 805306368 | bytes 4784128 | tf_op jit(solution)/shard_map/dot_general | solution.py:56
  51.7 67.1 %reduce-scatter.5.cloned.1.call-done = f32[512,32]{0,1:T(8,128)} async-done(((f32[4096,32]{0,1:T(8,128)}), f32[512,32]{0,1:T(8,128)}) %reduce-scatter.5.cloned.1.call-update) | async-done | bytes 65552 | tf_op jit(solution)/shard_map/reduce_scatter | solution.py:55
  121.1 1.5 collective-permute-done.1
  124.8 24.7 %all_gather.16 = f32[16,4096]{1,0:T(8,128)S(1)} all-gather(f32[16,512]{1,0:T(8,128)S(1)} %slice_add_fusion.1), channel_id=1, replica_groups=mesh['leaf'=4,'panel'=8] {'panel'}, dimensions={1}, use_global_device_ids=true | all-gather | bytes 294912 | tf_op jit(solution)/shard_map/all_gather | solution.py:49
  149.6 5.5 %fusion.4 = f32[16,512]{1,0:T(8,128)S(1)} fusion(f32[16,4096]{1,0:T(8,128)S(1)} %all_gather.16, bf16[2,1,512,4096]{3,2,1,0:T(8,128)(2,1)} %param.8), kind=kOutput, calls=%fused_computation.8 | convolution fusion | flops 402653184 | bytes 4489216 | tf_op jit(solution)/shard_map/dot_general | solution.py:48
  155.1 6.3 %convolution_bitcast_fusion.3 = f32[4096,16]{0,1:T(8,128)} fusion(f32[16,512]{1,0:T(8,128)S(1)} %fusion.4, bf16[2,1,4096,512]{3,2,1,0:T(8,128)(2,1)} %param.9), kind=kOutput, calls=%fused_computation.3 | convolution fusion | flops 402653184 | bytes 4489216 | tf_op jit(solution)/shard_map/dot_general | solution.py:56
  161.5 67.8 %reduce-scatter.7.cloned.1.call-done = f32[512,16]{0,1:T(8,128)} async-done(((f32[4096,16]{0,1:T(8,128)}), f32[512,16]{0,1:T(8,128)}) %reduce-scatter.7.cloned.1.call-update) | async-done | bytes 32784 | tf_op jit(solution)/shard_map/reduce_scatter | solution.py:55
  230.1 25.2 %all_gather.17 = f32[16,4096]{1,0:T(8,128)S(1)} all-gather(f32[16,512]{1,0:T(8,128)S(1)} %slice_subtract_fusion.1), channel_id=1, replica_groups=mesh['leaf'=4,'panel'=8] {'panel'}, dimensions={1}, use_global_device_ids=true | all-gather | bytes 294912 | tf_op jit(solution)/shard_map/all_gather | solution.py:67
  255.2 5.5 %fusion.60 = f32[16,512]{1,0:T(8,128)S(1)} fusion(f32[16,4096]{1,0:T(8,128)S(1)} %all_gather.17, bf16[512,4096]{1,0:T(8,128)(2,1)} %param.11), kind=kOutput, calls=%fused_computation.83 | convolution fusion | flops 402653184 | bytes 4489216 | tf_op jit(solution)/shard_map/dot_general | solution.py:66
  260.7 24.4 %all_gather.18 = f32[16,4096]{1,0:T(8,128)S(1)} all-gather(f32[16,512]{1,0:T(8,128)S(1)} %fusion.60), channel_id=1, replica_groups=mesh['leaf'=4,'panel'=8] {'panel'}, dimensions={1}, use_global_device_ids=true | all-gather | bytes 294912 | tf_op jit(solution)/shard_map/all_gather | solution.py:80
  285.2 3.9 fusion.31
  289.1 4.7 convolution_bitcast_fusion.2
  293.8 72.5 %reduce-scatter.9.cloned.1.call-done = f32[512,16]{0,1:T(8,128)} async-done(((f32[4096,16]{0,1:T(8,128)}), f32[512,16]{0,1:T(8,128)}) %reduce-scatter.9.cloned.1.call-update) | async-done | bytes 32784 | tf_op jit(solution)/shard_map/reduce_scatter | solution.py:86
  366.3 2.8 fusion.12
  370.4 1.6 collective-permute-done.2
  372.1 25.7 %all_gather.19 = f32[32,4096]{1,0:T(8,128)S(1)} all-gather(f32[32,512]{1,0:T(8,128)S(1)} %select_n.121), channel_id=1, replica_groups=mesh['leaf'=4,'panel'=8] {'panel'}, dimensions={1}, use_global_device_ids=true | all-gather | bytes 589824 | tf_op jit(solution)/shard_map/all_gather | solution.py:80
  397.7 4.3 fusion.28
  402.0 5.1 %convolution_bitcast_fusion = f32[4096,32]{0,1:T(8,128)} fusion(f32[32,512]{1,0:T(8,128)S(1)} %fusion.28, bf16[2,1,512,4096]{3,2,1,0:T(8,128)(2,1)} %param.8), kind=kOutput, calls=%fused_computation | convolution fusion | flops 805306368 | bytes 4784128 | tf_op jit(solution)/shard_map/dot_general | solution.py:87
  407.2 68.5 %reduce-scatter.11.cloned.1.call-done = f32[512,32]{0,1:T(8,128)} async-done(((f32[4096,32]{0,1:T(8,128)}), f32[512,32]{0,1:T(8,128)}) %reduce-scatter.11.cloned.1.call-update) | async-done | bytes 65552 | tf_op jit(solution)/shard_map/reduce_scatter | solution.py:86
  475.7 3.0 fusion.14
  478.7 2.6 collective-permute-start.3
  (40 shorter events, 12.5 us)
Async XLA Ops:
  7.2 111.6 %reduce-scatter.5.cloned.1.call-start = ((), (), s32[]{:S(2)}) async-start(), calls=%async_computation.4 | async-start | bytes 589824 | tf_op jit(solution)/shard_map/reduce_scatter | solution.py:55
  8.3 1.3 collective-permute-start
  51.6 177.7 %reduce-scatter.7.cloned.1.call-start = ((), (), s32[]{:S(2)}) async-start(), calls=%async_computation.5 | async-start | bytes 294912 | tf_op jit(solution)/shard_map/reduce_scatter | solution.py:55
  119.8 2.8 collective-permute-start.1
  161.4 204.9 %reduce-scatter.9.cloned.1.call-start = ((), (), s32[]{:S(2)}) async-start(), calls=%async_computation.6 | async-start | bytes 294912 | tf_op jit(solution)/shard_map/reduce_scatter | solution.py:86
  293.8 181.9 %reduce-scatter.11.cloned.1.call-start = ((), (), s32[]{:S(2)}) async-start(), calls=%async_computation.7 | async-start | bytes 589824 | tf_op jit(solution)/shard_map/reduce_scatter | solution.py:86
  369.1 2.8 collective-permute-start.2
  402.0 79.3 %copy-start = (f32[512,16]{0,1:T(8,128)S(1)}, f32[512,16]{0,1:T(8,128)}, u32[]{:S(2)}) copy-start(f32[512,16]{0,1:T(8,128)} %reduce-scatter.9.cloned.1.call-done) | copy-start | bytes 98308
  478.7 4.1 collective-permute-start.3
Sparse Core Ops, SparseCore 0:
  51.7 67.0 reduce-scatter.4
  161.5 67.7 reduce-scatter.6
  293.9 72.3 reduce-scatter.8
  407.3 68.3 reduce-scatter.10
where the time goes:
time: 491 us; the launch traced here: 490 us
  waiting for transfers between devices  280 us (57%)
  blocking collectives  127 us (26%)
  matrix products  56.8 us (12%)
  between operations  13.9 us (3%)
  starting transfers between devices  5.46 us (1%)
  other arithmetic  4.96 us (1%)
    reduce_scatter x2, waiting for transfers between devices, local(): lax.psum_scatter(lax.dot_general(pivot_inverse_cols, residual_part, CONTR...  141 us
    reduce_scatter x2, waiting for transfers between devices, local(): lax.psum_scatter(lax.dot_general(factor_rows, solved, CONTRACT_LAST, prec...  135 us
    all_gather x2, blocking collectives, local(): lax.all_gather(right_side, 'panel', axis=1, tiled=True)  51.6 us
    all_gather x2, blocking collectives, local(): lax.all_gather(known, 'panel', axis=1, tiled=True)  50.1 us
    all_gather x1, blocking collectives, local(): lax.all_gather(current, 'panel', axis=1, tiled=True)  25.2 us
    dot_general x2, matrix products, local(): lax.dot_general(factor_rows, solved, CONTRACT_LAST, precision=HIGHEST_PRE...  12.9 us
    dot_general x2, matrix products, local(): lax.dot_general(lax.all_gather(right_side, 'panel', axis=1, tiled=True),...  11.4 us
  transfers between devices with their start and end apart: 8, of which 7 were waited for; matrix products, arithmetic and copies ran while one was open for 0% of the time, Pallas kernels for 0%

commit v1 on v0

--- a/solution.py
+++ b/solution.py
@@ -6,6 +6,18 @@
 HIGHEST_PRECISION = lax.Precision.HIGHEST
 CONTRACT_LAST = (((1,), (1,)), ((), ()))
 CONTRACT_FIRST_LAST = (((0,), (1,)), ((), ()))
+
+
+def collect(x, axis, dim):
+    ways, here, hop = (lax.axis_size(axis), lax.axis_index(axis), x.shape[dim])
+    line, have = (x, 1)
+    while have < ways:
+        line = jnp.concatenate(
+            [line, lax.ppermute(line, axis, [(d, (d - have) % ways) for d in range(ways)])],
+            axis=dim,
+        )
+        have = 2 * have
+    return jnp.roll(line, here * hop, axis=dim)
 
 
 def partner(value, axis, stride):
@@ -46,7 +58,7 @@
         update_cols = lower_update[tree_level, 0]
         inverse_cols = inverse_rows.astype(jnp.float32)
         solved = lax.dot_general(
-            lax.all_gather(right_side, "panel", axis=1, tiled=True),
+            collect(right_side, "panel", 1),
             inverse_cols,
             CONTRACT_LAST,
             precision=HIGHEST_PRECISION,

time: 491 us -> 473 us (0.963)
  blocking collectives: 127 us -> 75.3 us
  waiting for transfers between devices: 280 us -> 301 us
  starting transfers between devices: 5.46 us -> 16.5 us
    all_gather x2 -> x0, blocking collectives: 51.6 us -> none  [local(): lax.all_gather(right_side, 'panel', axis=1, tiled=True)]
    ppermute x0 -> x6, waiting for transfers between devices: none -> 27 us  [collect(): lax.ppermute(line, axis, [(d, (d - have) % ways) for d in range(ways)])]
    ppermute x0 -> x6, starting transfers between devices: none -> 11 us  [collect(): lax.ppermute(line, axis, [(d, (d - have) % ways) for d in range(ways)])]
    reduce_scatter x2, waiting for transfers between devices: 135 us -> 130 us  [local(): lax.psum_scatter(lax.dot_general(factor_rows, solved, CONTRACT_LAST, prec...]
  transfers between devices with their start and end apart: 8 -> 14, of which waited for: 7 -> 13; matrix products, arithmetic and copies ran while one was open for 0% -> 0% of each run, Pallas kernels for 0% -> 0%
where the time goes in v1:
time: 473 us; the launch traced here: 472 us
  waiting for transfers between devices  301 us (64%)
  blocking collectives  75.3 us (16%)
  matrix products  56.8 us (12%)
  starting transfers between devices  16.5 us (3%)
  between operations  14.1 us (3%)
  other arithmetic  5 us (1%)
    reduce_scatter x2, waiting for transfers between devices, local(): lax.psum_scatter(lax.dot_general(pivot_inverse_cols, residual_part, CONTR...  141 us
    reduce_scatter x2, waiting for transfers between devices, local(): lax.psum_scatter(lax.dot_general(factor_rows, solved, CONTRACT_LAST, prec...  130 us
    all_gather x2, blocking collectives, local(): lax.all_gather(known, 'panel', axis=1, tiled=True)  50.2 us
    ppermute x6, waiting for transfers between devices, collect(): lax.ppermute(line, axis, [(d, (d - have) % ways) for d in range(ways)])  27 us
    all_gather x1, blocking collectives, local(): lax.all_gather(current, 'panel', axis=1, tiled=True)  25.1 us
    dot_general x2, matrix products, local(): lax.dot_general(factor_rows, solved, CONTRACT_LAST, precision=HIGHEST_PRE...  12.9 us
    dot_general x2, matrix products, local(): lax.dot_general(collect(right_side, 'panel', 1), inverse_cols, CONTRACT_L...  11.4 us
    ppermute x6, starting transfers between devices, collect(): lax.ppermute(line, axis, [(d, (d - have) % ways) for d in range(ways)])  11 us
  transfers between devices with their start and end apart: 14, of which 13 were waited for; matrix products, arithmetic and copies ran while one was open for 0% of the time, Pallas kernels for 0%

profile of v1, /device:TPU:1, one launch (start us, length us, event | category | flops | bytes accessed | tf_op | source)
XLA Modules:
  0.0 471.9 jit_solution(6415908847836129126)
XLA Ops:
  12.2 5.5 %collective-permute-start.1 = (f32[32,512]{1,0:T(8,128)S(1)}, f32[32,512]{1,0:T(8,128)S(1)}, u32[]{:S(2)}, u32[]{:S(2)}) collective-permute-start(f32[32,512]{1,0:T(8,128)S(1)} %get-tuple-element.5), channel_id=1, source_target_pairs={{0,7},{1,0},{2,1},{3,2},{4,3},{5,4},{6,5},{7,6},{8,15},{9,8},{10,9... | collective-permute-start | bytes 196616 | tf_op jit(solution)/shard_map/ppermute | solution.py:16
  19.9 3.0 collective-permute-done.2
  23.0 14.3 %collective-permute-done.3 = f32[32,2048]{1,0:T(8,128)S(1)} collective-permute-done((f32[32,2048]{1,0:T(8,128)S(1)}, f32[32,2048]{1,0:T(8,128)S(1)}, u32[]{:S(2)}, u32[]{:S(2)}) %collective-permute-start.3) | collective-permute-done | bytes 262176 | tf_op jit(solution)/shard_map/ppermute | solution.py:16
  37.4 5.9 %fusion.10 = f32[32,512]{1,0:T(8,128)S(1)} fusion(bf16[2,1,512,4096]{3,2,1,0:T(8,128)(2,1)} %param.8, f32[32,8192]{1,0:T(8,128)S(1)} %constant_dynamic-update-slice_fusion, s32[]{:T(128)S(6)} %select_n.129), kind=kOutput, calls=%fused_computation.14 | convolution fusion | flops 805306368 | bytes 4784132 | tf_op jit(solution)/shard_map/dot_general | solution.py:60
  43.3 6.7 %convolution_bitcast_fusion.1 = f32[4096,32]{0,1:T(8,128)} fusion(f32[32,512]{1,0:T(8,128)S(1)} %fusion.10, bf16[2,1,4096,512]{3,2,1,0:T(8,128)(2,1)} %param.9), kind=kOutput, calls=%fused_computation.1 | convolution fusion | flops 805306368 | bytes 4784128 | tf_op jit(solution)/shard_map/dot_general | solution.py:68
  50.1 62.6 %reduce-scatter.5.cloned.1.call-done = f32[512,32]{0,1:T(8,128)} async-done(((f32[4096,32]{0,1:T(8,128)}), f32[512,32]{0,1:T(8,128)}) %reduce-scatter.5.cloned.1.call-update) | async-done | bytes 65552 | tf_op jit(solution)/shard_map/reduce_scatter | solution.py:67
  118.7 2.3 collective-permute-start.5
  126.1 5.6 %collective-permute-done.7 = f32[16,2048]{1,0:T(8,128)S(1)} collective-permute-done((f32[16,2048]{1,0:T(8,128)S(1)}, f32[16,2048]{1,0:T(8,128)S(1)}, u32[]{:S(2)}, u32[]{:S(2)}) %collective-permute-start.7) | collective-permute-done | bytes 131104 | tf_op jit(solution)/shard_map/ppermute | solution.py:16
  131.8 5.5 %fusion.4 = f32[16,512]{1,0:T(8,128)S(1)} fusion(bf16[2,1,512,4096]{3,2,1,0:T(8,128)(2,1)} %param.8, f32[16,8192]{1,0:T(8,128)S(1)} %constant_dynamic-update-slice_fusion.8, s32[]{:T(128)S(6)} %select_n.129), kind=kOutput, calls=%fused_computation.8 | convolution fusion | flops 402653184 | bytes 4489220 | tf_op jit(solution)/shard_map/dot_general | solution.py:60
  137.3 6.3 %convolution_bitcast_fusion.3 = f32[4096,16]{0,1:T(8,128)} fusion(f32[16,512]{1,0:T(8,128)S(1)} %fusion.4, bf16[2,1,4096,512]{3,2,1,0:T(8,128)(2,1)} %param.9), kind=kOutput, calls=%fused_computation.3 | convolution fusion | flops 402653184 | bytes 4489216 | tf_op jit(solution)/shard_map/dot_general | solution.py:68
  143.6 67.3 %reduce-scatter.7.cloned.1.call-done = f32[512,16]{0,1:T(8,128)} async-done(((f32[4096,16]{0,1:T(8,128)}), f32[512,16]{0,1:T(8,128)}) %reduce-scatter.7.cloned.1.call-update) | async-done | bytes 32784 | tf_op jit(solution)/shard_map/reduce_scatter | solution.py:67
  211.7 25.1 %all_gather.9 = f32[16,4096]{1,0:T(8,128)S(1)} all-gather(f32[16,512]{1,0:T(8,128)S(1)} %slice_subtract_fusion.1), channel_id=1, replica_groups=mesh['leaf'=4,'panel'=8] {'panel'}, dimensions={1}, use_global_device_ids=true | all-gather | bytes 294912 | tf_op jit(solution)/shard_map/all_gather | solution.py:79
  236.8 5.5 %fusion.64 = f32[16,512]{1,0:T(8,128)S(1)} fusion(f32[16,4096]{1,0:T(8,128)S(1)} %all_gather.9, bf16[512,4096]{1,0:T(8,128)(2,1)} %param.11), kind=kOutput, calls=%fused_computation.107 | convolution fusion | flops 402653184 | bytes 4489216 | tf_op jit(solution)/shard_map/dot_general | solution.py:78
  242.4 24.5 %all_gather.10 = f32[16,4096]{1,0:T(8,128)S(1)} all-gather(f32[16,512]{1,0:T(8,128)S(1)} %fusion.64), channel_id=1, replica_groups=mesh['leaf'=4,'panel'=8] {'panel'}, dimensions={1}, use_global_device_ids=true | all-gather | bytes 294912 | tf_op jit(solution)/shard_map/all_gather | solution.py:92
  266.8 3.9 fusion.31
  270.7 4.7 convolution_bitcast_fusion.2
  275.5 72.3 %reduce-scatter.9.cloned.1.call-done = f32[512,16]{0,1:T(8,128)} async-done(((f32[4096,16]{0,1:T(8,128)}), f32[512,16]{0,1:T(8,128)}) %reduce-scatter.9.cloned.1.call-update) | async-done | bytes 32784 | tf_op jit(solution)/shard_map/reduce_scatter | solution.py:98
  347.8 2.8 fusion.12
  353.6 25.7 %all_gather.11 = f32[32,4096]{1,0:T(8,128)S(1)} all-gather(f32[32,512]{1,0:T(8,128)S(1)} %select_n.142), channel_id=1, replica_groups=mesh['leaf'=4,'panel'=8] {'panel'}, dimensions={1}, use_global_device_ids=true | all-gather | bytes 589824 | tf_op jit(solution)/shard_map/all_gather | solution.py:92
  379.2 4.3 fusion.28
  383.5 5.2 %convolution_bitcast_fusion = f32[4096,32]{0,1:T(8,128)} fusion(f32[32,512]{1,0:T(8,128)S(1)} %fusion.28, bf16[2,1,512,4096]{3,2,1,0:T(8,128)(2,1)} %param.8), kind=kOutput, calls=%fused_computation | convolution fusion | flops 805306368 | bytes 4784128 | tf_op jit(solution)/shard_map/dot_general | solution.py:99
  388.7 68.6 %reduce-scatter.11.cloned.1.call-done = f32[512,32]{0,1:T(8,128)} async-done(((f32[4096,32]{0,1:T(8,128)}), f32[512,32]{0,1:T(8,128)}) %reduce-scatter.11.cloned.1.call-update) | async-done | bytes 65552 | tf_op jit(solution)/shard_map/reduce_scatter | solution.py:98
  457.3 3.0 fusion.14
  460.4 2.6 collective-permute-start.9
  (68 shorter events, 24.8 us)
Async XLA Ops:
  7.2 105.5 %reduce-scatter.5.cloned.1.call-start = ((), (), s32[]{:S(2)}) async-start(), calls=%async_computation.4 | async-start | bytes 589824 | tf_op jit(solution)/shard_map/reduce_scatter | solution.py:67
  8.3 1.3 collective-permute-start
  12.2 6.8 %collective-permute-start.1 = (f32[32,512]{1,0:T(8,128)S(1)}, f32[32,512]{1,0:T(8,128)S(1)}, u32[]{:S(2)}, u32[]{:S(2)}) collective-permute-start(f32[32,512]{1,0:T(8,128)S(1)} %get-tuple-element.5), channel_id=1, source_target_pairs={{0,7},{1,0},{2,1},{3,2},{4,3},{5,4},{6,5},{7,6},{8,15},{9,8},{10,9... | collective-permute-start | bytes 196616 | tf_op jit(solution)/shard_map/ppermute | solution.py:16
  19.0 3.9 collective-permute-start.2
  22.9 14.5 %collective-permute-start.3 = (f32[32,2048]{1,0:T(8,128)S(1)}, f32[32,2048]{1,0:T(8,128)S(1)}, u32[]{:S(2)}, u32[]{:S(2)}) collective-permute-start(f32[32,2048]{1,0:T(8,128)S(1)} %pad_maximum_fusion), channel_id=1, source_target_pairs={{0,4},{1,5},{2,6},{3,7},{4,0},{5,1},{6,2},{7,3},{8,12},{9,13},{10,... | collective-permute-start | bytes 786440 | tf_op jit(solution)/shard_map/ppermute | solution.py:16
  50.0 160.9 %reduce-scatter.7.cloned.1.call-start = ((), (), s32[]{:S(2)}) async-start(), calls=%async_computation.5 | async-start | bytes 294912 | tf_op jit(solution)/shard_map/reduce_scatter | solution.py:67
  113.6 2.8 collective-permute-start.4
  118.7 3.3 collective-permute-start.5
  122.0 3.1 collective-permute-start.6
  125.1 6.6 %collective-permute-start.7 = (f32[16,2048]{1,0:T(8,128)S(1)}, f32[16,2048]{1,0:T(8,128)S(1)}, u32[]{:S(2)}, u32[]{:S(2)}) collective-permute-start(f32[16,2048]{1,0:T(8,128)S(1)} %pad_maximum_fusion.2), channel_id=1, source_target_pairs={{0,4},{1,5},{2,6},{3,7},{4,0},{5,1},{6,2},{7,3},{8,12},{9,13},{10,... | collective-permute-start | bytes 393224 | tf_op jit(solution)/shard_map/ppermute | solution.py:16
  143.6 204.2 %reduce-scatter.9.cloned.1.call-start = ((), (), s32[]{:S(2)}) async-start(), calls=%async_computation.6 | async-start | bytes 294912 | tf_op jit(solution)/shard_map/reduce_scatter | solution.py:98
  275.4 181.9 %reduce-scatter.11.cloned.1.call-start = ((), (), s32[]{:S(2)}) async-start(), calls=%async_computation.7 | async-start | bytes 589824 | tf_op jit(solution)/shard_map/reduce_scatter | solution.py:98
  350.6 2.8 collective-permute-start.8
  383.5 79.5 %copy-start = (f32[512,16]{0,1:T(8,128)S(1)}, f32[512,16]{0,1:T(8,128)}, u32[]{:S(2)}) copy-start(f32[512,16]{0,1:T(8,128)} %reduce-scatter.9.cloned.1.call-done) | copy-start | bytes 98308
  460.4 4.1 collective-permute-start.9
Sparse Core Ops, SparseCore 0:
  50.1 62.4 reduce-scatter.4
  143.7 67.1 reduce-scatter.6
  275.5 72.2 reduce-scatter.8
  388.8 68.4 reduce-scatter.10
